TPU v7x, 32 devices: a whole 2x2x4 slice. The times are simulated.
32 devices in a mesh: groups: 2 (over y), rows: 8 (over z, x), sub: 2 (over core).
Axes of the slice: x: 2, y: 2, z: 4, core: 2. Of those that a mesh axis runs over, the one named last changes fastest.
Arguments:
- residuals: bfloat16 [2048, 2048], P(('groups', 'rows'), 'sub'), parts along dimension 0, may hold values from -96 to 96
- codes: int32 [2048, 256], P(('groups', 'rows'), 'sub'), parts along dimension 0, may hold values from 0 to 127
- codebook: float32 [512, 8, 128], P(('groups', 'sub')), parts along dimension 0, may hold values from -4 to 4
Outputs:
- refined: float32 [512, 8, 128], P(('groups', 'sub')), parts along dimension 0
There are 2 independent parts, one for each index of `groups`. A program takes and returns all parts, laid end to end along the dimension named above; each array names one. Nothing has to cross between parts.
All inputs are finite; a program needn't handle non-finite values.
Results may differ from a plain program's by a relative error of at most 0.0037.
Values sent between devices are 32-bit elements; how exact they have to be, the bound alone decides.
A program may use at most 64 MiB of HBM per device.

v0:
```python
import jax
import jax.numpy as jnp
from jax import lax
from jax.sharding import PartitionSpec as P


def renew(prior, sums, counts, lam):
    all_sums, all_counts = lax.psum((sums, counts), "rows")
    return (all_sums + lam * prior) / (all_counts[:, None, :] + lam)


def shards(residuals, codes, codebook):
    row_count = residuals.shape[0]
    local = codes.shape[1]
    subdim = residuals.shape[1] // local
    width = codebook.shape[2]
    span = 16
    turns = local // span
    lam = row_count * lax.axis_size("rows") / (8.0 * width)
    levels = jnp.arange(width, dtype=jnp.int32)
    order = jnp.arange(turns, dtype=jnp.int32)
    columns = residuals.reshape(row_count, local, subdim).transpose(1, 2, 0)
    labels = codes.T

    def block_of(turn):
        return lax.dynamic_slice_in_dim(columns, turn * span, span, 0)

    def first(turn):
        piece = block_of(turn)
        label = lax.dynamic_slice_in_dim(labels, turn * span, span, 0)
        onehot = (label[:, :, None] == levels[None, None, :]).astype(jnp.bfloat16)
        sums = jnp.einsum("gdr,grk->gdk", piece, onehot, preferred_element_type=jnp.float32)
        return (sums, jnp.sum(onehot, axis=1, dtype=jnp.float32))

    sums1, counts1 = lax.map(first, order)
    book1 = renew(codebook, sums1.reshape(local, subdim, width), counts1.reshape(local, width), lam)

    def second(turn):
        piece = block_of(turn)
        center = lax.dynamic_slice_in_dim(book1, turn * span, span, 0)
        cross = jnp.einsum(
            "gdr,gdk->grk", piece, center.astype(jnp.bfloat16), preferred_element_type=jnp.float32
        )
        scores = 2.0 * cross - jnp.sum(center * center, axis=1)[:, None, :]
        weights = jax.nn.softmax(scores, axis=-1).astype(jnp.bfloat16)
        sums = jnp.einsum("gdr,grk->gdk", piece, weights, preferred_element_type=jnp.float32)
        return (sums, jnp.sum(weights, axis=1, dtype=jnp.float32))

    sums2, counts2 = lax.map(second, order)
    return renew(book1, sums2.reshape(local, subdim, width), counts2.reshape(local, width), lam)


def solution(mesh):
    in_specs = (
        P(("groups", "rows"), "sub"),
        P(("groups", "rows"), "sub"),
        P(("groups", "sub"), None, None),
    )
    out_specs = P(("groups", "sub"), None, None)
    return jax.shard_map(shards, mesh=mesh, in_specs=in_specs, out_specs=out_specs, check_vma=False)
```

profile of v0, /device:TPU:0, one launch (start us, length us, event | category | flops | bytes accessed | tf_op | source)
XLA Modules:
  0.0 210.2 jit_solution(2224105033658863860)
XLA Ops:
  6.5 1.1 copy.5
  7.9 19.4 %while.26 = (s32[]{:T(128)}, f32[8,16,8,128]{3,2,1,0:T(8,128)S(1)}, f32[8,16,128]{2,1,0:T(8,128)S(1)}, s32[8]{0:T(128)S(1)}, bf16[128,8,128]{2,1,0:T(8,128)(2,1)...) while((s32[]{:T(128)}, f32[8,16,8,128]{3,2,1,0:T(8,128)S(1)}, ...), condition=%wide.region_2.3_spmd.clone, body=%wide.region_0.2_spmd.clone.sunk | while | flops 5502982 | bytes 155823 | solution.py:35
  7.9 0.7 dynamic_slice.58
  9.3 0.7 fusion.41
  10.3 0.7 dynamic_slice.58
  11.7 0.7 fusion.41
  12.7 0.7 dynamic_slice.58
  14.1 0.7 fusion.41
  15.2 0.7 dynamic_slice.58
  16.6 0.7 fusion.41
  17.6 0.7 dynamic_slice.58
  19.0 0.7 fusion.41
  20.0 0.7 dynamic_slice.58
  22.5 0.7 dynamic_slice.58
  24.9 0.7 dynamic_slice.58
  27.3 0.8 copy-done.1
  28.2 76.1 %all-reduce.7.cloned.1.call-done = (f32[128,8,128]{2,1,0:T(8,128)}, f32[128,128]{1,0:T(8,128)}) async-done(((f32[128,8,128]{2,1,0:T(8,128)}, f32[128,128]{1,0:T(8,128)}), (f32[128,8,128]{2,1,0:T(8,128)}, f32[128,128]{1,0:T(8,128)})) %all-reduce.7.cloned.1.call-update) | async-done | bytes 589840 | tf_op jit(solution)/shard_map/psum | solution.py:8
  104.3 0.8 broadcast_add_fusion.1
  105.2 1.1 add_divide_fusion.1
  106.3 20.8 %while.25 = (s32[]{:T(128)}, f32[8,16,8,128]{3,2,1,0:T(8,128)S(1)}, f32[8,16,128]{2,1,0:T(8,128)S(1)}, s32[8]{0:T(128)S(1)}, bf16[128,8,128]{2,1,0:T(8,128)(2,1)...) while((s32[]{:T(128)}, f32[8,16,8,128]{3,2,1,0:T(8,128)S(1)}, ...), condition=%wide.region_10.11_spmd, body=%wide.region_5.10_spmd.sunk | while | flops 10514565 | bytes 3433647 | solution.py:49
  127.2 0.8 copy-done
  128.0 72.6 %all-reduce.5.cloned.1.call-done = (f32[128,8,128]{2,1,0:T(8,128)}, f32[128,128]{1,0:T(8,128)}) async-done(((f32[128,8,128]{2,1,0:T(8,128)}, f32[128,128]{1,0:T(8,128)}), (f32[128,8,128]{2,1,0:T(8,128)}, f32[128,128]{1,0:T(8,128)})) %all-reduce.5.cloned.1.call-update) | async-done | bytes 589840 | tf_op jit(solution)/shard_map/psum | solution.py:8
  200.6 0.8 broadcast_add_fusion
  201.4 1.9 add_divide_fusion
  (96 shorter events, 20.7 us)
Async XLA Ops:
  6.5 1.2 copy-start.5
  6.5 97.8 %all-reduce.7.cloned.1.call-start = ((), (), s32[]{:S(2)}) async-start(), calls=%async_computation.1 | async-start | bytes 1179648 | tf_op jit(solution)/shard_map/psum | solution.py:8
  27.3 0.8 copy-start.1
  27.3 0.8 copy-start.4
  27.3 77.8 %copy-start.2 = (f32[128,8,128]{2,1,0:T(8,128)S(1)}, f32[128,8,128]{2,1,0:T(8,128)}, u32[]{:S(2)}) copy-start(f32[128,8,128]{2,1,0:T(8,128)} %param.9) | copy-start | bytes 1572868
  28.1 172.5 %all-reduce.5.cloned.1.call-start = ((), (), s32[]{:S(2)}) async-start(), calls=%async_computation | async-start | bytes 1179648 | tf_op jit(solution)/shard_map/psum | solution.py:8
  127.2 0.8 copy-start
  127.2 0.8 copy-start.3
Sparse Core Ops, SparseCore 0:
  28.3 75.9 all-reduce.6
  128.1 72.4 all-reduce.4
where the time goes:
time: 211 us; the launch traced here: 210 us
  waiting for transfers between devices  149 us (71%)
  between operations  13.5 us (6%)
  local copies, waits for them, and re-layouts  13.2 us (6%)
  matrix products  12.8 us (6%)
  loops' own time  11.3 us (5%)
  other arithmetic  10.6 us (5%)
    psum x2, waiting for transfers between devices, renew(): all_sums, all_counts = lax.psum((sums, counts), 'rows')  149 us
    dynamic_slice x16, local copies, waits for them, and re-layouts, shards(): sums1, counts1 = lax.map(first, order)  10.1 us
    another operation x1, loops' own time, shards(): sums1, counts1 = lax.map(first, order)  5.91 us
    another operation x1, loops' own time, shards(): sums2, counts2 = lax.map(second, order)  5.39 us
    dot_general x8, matrix products, first(): jnp.einsum('gdr,grk->gdk', piece, onehot, preferred_element_type=jnp.floa...  5.23 us
    sub x8, matrix products, second(): weights = jax.nn.softmax(scores, axis=-1).astype(jnp.bfloat16)  4.64 us
  transfers between devices with their start and end apart: 2, of which 2 were waited for; matrix products, arithmetic and copies ran while one was open for 0% of the time, Pallas kernels for 0%

commit v1 on v0

v1 whole, which is shorter than its diff:
```python
import functools

import jax
import jax.numpy as jnp
from jax import lax
from jax.experimental import pallas as pl
from jax.experimental.pallas import tpu as pltpu
from jax.sharding import PartitionSpec as P


def kernel(n, gs, groups, lam, tile, x_ref, c_ref, cb_ref, o_ref,
           xs, xr, cb, res, send_x, recv_x, send_o, recv_o, own, cb_sem):
    rows, width = x_ref.shape[0], cb_ref.shape[-1]
    me = lax.axis_index("rows")
    subdim = cb_ref.shape[2] // gs
    per = gs * groups
    span = gs * subdim

    barrier = pltpu.get_barrier_semaphore()

    def greet(k, _):
        pl.semaphore_signal(barrier, inc=1, device_id={"rows": lax.rem(me + k, n)},
                            device_id_type=pl.DeviceIdType.MESH)
        return 0

    lax.fori_loop(1, n, greet, 0)
    prior = pltpu.make_async_copy(cb_ref.at[me], cb, cb_sem)
    prior.start()

    flipped = x_ref[...].astype(jnp.float32).T
    labels = c_ref[...].astype(jnp.float32).T
    for j in range(n):
        for g in range(groups):
            at = j * per + g * gs
            xs[j, g, :span, :] = flipped[at * subdim:at * subdim + span]
            xs[j, g, span:span + gs, :] = labels[at:at + gs]
    xr[me] = xs[me]
    pl.semaphore_wait(barrier, n - 1)

    def block(source, target, g, slot):
        return pltpu.make_async_remote_copy(
            src_ref=xs.at[target, g], dst_ref=xr.at[source, g],
            send_sem=send_x.at[g, target], recv_sem=recv_x.at[g, slot],
            device_id={"rows": target}, device_id_type=pl.DeviceIdType.MESH)

    def result(source, target, g, slot):
        return pltpu.make_async_remote_copy(
            src_ref=res.at[g], dst_ref=o_ref.at[source, g],
            send_sem=send_o.at[g, target], recv_sem=recv_o.at[g, slot],
            device_id={"rows": target}, device_id_type=pl.DeviceIdType.MESH)

    def each_peer(act):
        def body(k, _):
            act(lax.rem(me + k, n))
            return 0
        lax.fori_loop(1, n, body, 0)

    for g in range(groups):
        each_peer(lambda p, g=g: block(me, p, g, me).start())
    prior.wait()

    level = lax.broadcasted_iota(jnp.int32, (width, tile * rows), 0).astype(jnp.float32)
    ones = jnp.ones((8, tile * rows), jnp.float32)

    def over_tiles(step):
        if n == tile:
            return step(0)
        return lax.fori_loop(
            0, n // tile, lambda t, total: total + step(t),
            jnp.zeros((subdim + 8, width), jnp.float32))

    for g in range(groups):
        each_peer(lambda p, g=g: block(p, p, g, p).wait_recv())

        def train(m, _, g=g):
            line = pl.multiple_of(m * subdim, subdim)

            def columns(t):
                parts = [xr[t * tile + s, g, pl.ds(line, subdim), :] for s in range(tile)]
                full = jnp.concatenate(parts, axis=1)
                return jnp.concatenate([full, ones], axis=0).astype(jnp.bfloat16)

            def reduce_rows(points, weights):
                return lax.dot_general(points, weights, (((1,), (1,)), ((), ())),
                                       preferred_element_type=jnp.float32)

            def first(t):
                code = jnp.concatenate(
                    [xr[t * tile + s, g, pl.ds(span + m, 1), :] for s in range(tile)], axis=1)
                onehot = (level == code).astype(jnp.float32).astype(jnp.bfloat16)
                return reduce_rows(columns(t), onehot)

            total = over_tiles(first)
            before = cb[g, pl.ds(line, subdim), :]
            book = (total[:subdim] + lam * before) / (total[subdim:subdim + 1] + lam)
            norm = -jnp.sum(book * book, axis=0, keepdims=True)
            high = norm.astype(jnp.bfloat16).astype(jnp.float32)
            middle = (norm - high).astype(jnp.bfloat16).astype(jnp.float32)
            low = norm - high - middle
            center = jnp.concatenate(
                [2.0 * book.astype(jnp.bfloat16).astype(jnp.float32), high, middle, low,
                 jnp.zeros((5, width), jnp.float32)], axis=0).T.astype(jnp.bfloat16)

            def second(t):
                points = columns(t)
                scores = jnp.dot(center, points, preferred_element_type=jnp.float32)
                top = jnp.max(scores, axis=0, keepdims=True)
                raised = jnp.exp(scores - top)
                share = 1.0 / jnp.sum(raised, axis=0, keepdims=True)
                return reduce_rows(points, (raised * share).astype(jnp.bfloat16))

            total = over_tiles(second)
            res[g, pl.ds(line, subdim), :] = (
                (total[:subdim] + lam * book) / (total[subdim:subdim + 1] + lam))
            return 0

        lax.fori_loop(0, gs, train, 0)
        each_peer(lambda p, g=g: result(me, p, g, me).start())
        pltpu.make_async_copy(res.at[g], o_ref.at[me, g], own.at[g]).start()

    for g in range(groups):
        each_peer(lambda p, g=g: block(me, p, g, me).wait_send())
        each_peer(lambda p, g=g: result(me, p, g, me).wait_send())
        each_peer(lambda p, g=g: result(p, p, g, p).wait_recv())
        pltpu.make_async_copy(res.at[g], o_ref.at[me, g], own.at[g]).wait()


def shards(residuals, codes, codebook):
    rows = residuals.shape[0]
    local, subdim, width = codebook.shape
    n = lax.axis_size("rows")
    per = local // n
    gs = 8 if per % 8 == 0 else per
    groups = per // gs
    lam = rows * n / (8.0 * width)
    tile = min(n, 8)
    span = gs * subdim
    lines = span + -(-gs // 8) * 8
    shape = (n, groups, span, width)
    out = pl.pallas_call(
        functools.partial(kernel, n, gs, groups, lam, tile),
        out_shape=jax.ShapeDtypeStruct(shape, jnp.float32),
        in_specs=[pl.BlockSpec(memory_space=pltpu.VMEM)] * 2 + [pl.BlockSpec(memory_space=pl.ANY)],
        out_specs=pl.BlockSpec(memory_space=pl.ANY),
        scratch_shapes=[
            pltpu.VMEM((n, groups, lines, rows), jnp.float32),
            pltpu.VMEM((n, groups, lines, rows), jnp.float32),
            pltpu.VMEM((groups, span, width), jnp.float32),
            pltpu.VMEM((groups, span, width), jnp.float32),
            pltpu.SemaphoreType.DMA((groups, n)),
            pltpu.SemaphoreType.DMA((groups, n)),
            pltpu.SemaphoreType.DMA((groups, n)),
            pltpu.SemaphoreType.DMA((groups, n)),
            pltpu.SemaphoreType.DMA((groups,)),
            pltpu.SemaphoreType.DMA,
        ],
        compiler_params=pltpu.CompilerParams(collective_id=0, has_side_effects=True),
        name="lloyd",
    )(residuals, codes, codebook.reshape(shape))
    return out.reshape(local, subdim, width)


def solution(mesh):
    in_specs = (
        P(("groups", "rows"), "sub"),
        P(("groups", "rows"), "sub"),
        P(("groups", "sub"), None, None),
    )
    out_specs = P(("groups", "sub"), None, None)
    return jax.shard_map(shards, mesh=mesh, in_specs=in_specs, out_specs=out_specs, check_vma=False)
```

time: 211 us -> 38.3 us (0.18)
  waiting for transfers between devices: 149 us -> 0 us
  Pallas kernels: 0 us -> 36.2 us
  between operations: 13.5 us -> 0.01 us
  matrix products: 12.8 us -> 0 us
  local copies, waits for them, and re-layouts: 13.2 us -> 1.87 us
  loops' own time: 11.3 us -> 0 us
  other arithmetic: 10.6 us -> 0 us
    psum x2 -> x0, waiting for transfers between devices: 149 us -> none  [renew(): all_sums, all_counts = lax.psum((sums, counts), 'rows')]
    pallas_call x0 -> x1, Pallas kernels: none -> 36.2 us  [shards(): pl.pallas_call(functools.partial(kernel, n, gs, groups, lam, tile), out_s...]
    another operation x2 -> x0, loops' own time: 11.3 us -> none  [the longest x1 5.91 us: shards(): sums1, counts1 = lax.map(first, order)]
    dynamic_slice x24 -> x0, local copies, waits for them, and re-layouts: 10.2 us -> none  [the longest x16 10.1 us: shards(): sums1, counts1 = lax.map(first, order)]
    dot_general x16 -> x0, matrix products: 8.18 us -> none  [the longest x8 5.23 us: first(): jnp.einsum('gdr,grk->gdk', piece, onehot, preferred_element_type=jnp.floa...]
    reduce_sum x24 -> x0, other arithmetic: 5.9 us -> none  [the longest x8 2.85 us: first(): return (sums, jnp.sum(onehot, axis=1, dtype=jnp.float32))]
    sub x8 -> x0, matrix products: 4.64 us -> none  [second(): weights = jax.nn.softmax(scores, axis=-1).astype(jnp.bfloat16)]
    div x2 -> x0, other arithmetic: 3.02 us -> none  [renew(): return (all_sums + lam * prior) / (all_counts[:, None, :] + lam)]
  transfers between devices with their start and end apart: 2 -> 0, of which waited for: 2 -> 0; matrix products, arithmetic and copies ran while one was open for 0% -> 0% of each run, Pallas kernels for 0% -> 0%
where the time goes in v1:
time: 38.3 us; the launch traced here: 38.1 us
  Pallas kernels  36.2 us (95%)
  local copies, waits for them, and re-layouts  1.87 us (5%)
    pallas_call x1, Pallas kernels, shards(): pl.pallas_call(functools.partial(kernel, n, gs, groups, lam, tile), out_s...  36.2 us
    unnamed x1, local copies, waits for them, and re-layouts  1.87 us

profile of v1, /device:TPU:0, one launch (start us, length us, event | category | flops | bytes accessed | tf_op | source)
XLA Modules:
  0.0 38.1 jit_solution(17701041535168746503)
XLA Ops:
  0.0 36.2 %lloyd.1 = f32[8,2,64,128]{3,2,1,0:T(8,128)} custom-call(bf16[128,1024]{1,0:T(8,128)(2,1)} %x_ref.1, s32[128,128]{1,0:T(8,128)} %c_ref.1, f32[8,2,64,128]{3,2,1,0:T(8,128)} %bitcast.3), custom_call_target="tpu_custom_call" | custom-call | tf_op jit(solution)/shard_map/lloyd/pallas_call | solution.py:140
  36.2 1.9 %copy.5 = f32[128,8,128]{2,1,0:T(8,128)} copy(f32[128,8,128]{2,1,0:T(8,128)} %bitcast.2) | data formatting | bytes 1048576

commit v2 on v0

v2 whole, which is shorter than its diff:
```python
import functools

import jax
import jax.numpy as jnp
from jax import lax
from jax.experimental import pallas as pl
from jax.experimental.pallas import tpu as pltpu
from jax.sharding import PartitionSpec as P

MESH = pl.DeviceIdType.MESH


def kernel(n, sizes, direct, lam, tile, x_hbm, c_hbm, cb_hbm, o_ref, x_ref, c_ref,
           xs, xr, cb, res, send_x, recv_x, send_o, recv_o, relay, own, in_sem):
    rows, width = x_ref.shape[0], cb.shape[-1]
    per = sum(sizes)
    subdim = cb.shape[0] // per
    base = xs.shape[1] - per * subdim
    starts = [sum(sizes[:g]) for g in range(len(sizes))]
    groups = range(len(sizes))
    side = 2 if n % 2 == 0 else 1
    levels = n // side
    me = lax.axis_index("rows")
    level, column = lax.div(me, side), lax.rem(me, side)

    barrier = pltpu.get_barrier_semaphore()

    def greet(k, _):
        pl.semaphore_signal(barrier, inc=1, device_id={"rows": lax.rem(me + k, n)},
                            device_id_type=MESH)
        return 0

    lax.fori_loop(1, n, greet, 0, unroll=n <= 8)
    loads = [pltpu.make_async_copy(x_hbm, x_ref, in_sem.at[0]),
             pltpu.make_async_copy(c_hbm, c_ref, in_sem.at[1]),
             pltpu.make_async_copy(cb_hbm.at[me], cb, in_sem.at[2])]
    for load in loads:
        load.start()
    loads[0].wait()
    flipped = x_ref[...].astype(jnp.float32).T
    for j in range(n):
        at = j * per * subdim
        xs[j, base:, :] = flipped[at:at + per * subdim]
    loads[1].wait()
    labels = c_ref[...].astype(jnp.float32).T
    for j in range(n):
        xs[j, :per, :] = labels[j * per:(j + 1) * per]
        if base > per:
            xs[j, per:base, :] = jnp.zeros((base - per, rows), jnp.float32)
    xr[me] = xs[me]
    loads[2].wait()
    pl.semaphore_wait(barrier, n - 1)

    def piece(g):
        first = 0 if g == 0 else base + starts[g] * subdim
        return pl.ds(first, base + (starts[g] + sizes[g]) * subdim - first)

    def lines(g):
        return pl.ds(starts[g] * subdim, sizes[g] * subdim)

    def block(source, target, g):
        return pltpu.make_async_remote_copy(
            src_ref=xs.at[target, piece(g)], dst_ref=xr.at[source, piece(g)],
            send_sem=send_x.at[g, target], recv_sem=recv_x.at[g, source],
            device_id={"rows": target}, device_id_type=MESH)

    def result(source, target, g):
        return pltpu.make_async_remote_copy(
            src_ref=res.at[lines(g)], dst_ref=o_ref.at[source, lines(g)],
            send_sem=send_o.at[g, target], recv_sem=recv_o.at[g, source],
            device_id={"rows": target}, device_id_type=MESH)

    def passed(source, g):
        return pltpu.make_async_remote_copy(
            src_ref=o_ref.at[source, lines(g)], dst_ref=o_ref.at[source, lines(g)],
            send_sem=relay.at[g, source], recv_sem=recv_o.at[g, source],
            device_id={"rows": level * side + 1 - column}, device_id_type=MESH)

    def kept(g):
        return pltpu.make_async_copy(res.at[lines(g)], o_ref.at[me, lines(g)], own.at[g])

    def each_peer(act):
        def body(k, _):
            act(lax.rem(me + k, n))
            return 0
        lax.fori_loop(1, n, body, 0, unroll=n <= 8)

    def each_level(first, where, act):
        def body(k, _):
            act(lax.rem(level + k, levels) * side + where)
            return 0
        lax.fori_loop(first, levels, body, 0, unroll=n <= 8)

    for g in groups:
        each_peer(lambda p, g=g: block(me, p, g).start())

    number = lax.broadcasted_iota(jnp.int32, (width, tile * rows), 0).astype(jnp.float32)
    ones = jnp.ones((8, tile * rows), jnp.float32)

    def over_tiles(step):
        if n == tile:
            return step(0)
        return lax.fori_loop(
            0, n // tile, lambda t, total: total + step(t),
            jnp.zeros((subdim + 8, width), jnp.float32))

    def reduce_rows(points, weights):
        return lax.dot_general(points, weights, (((1,), (1,)), ((), ())),
                               preferred_element_type=jnp.float32)

    def train(m, _):
        line = pl.multiple_of(m * subdim, subdim)

        def columns(t):
            parts = [xr[t * tile + s, pl.ds(base + line, subdim), :] for s in range(tile)]
            full = jnp.concatenate(parts, axis=1)
            return jnp.concatenate([full, ones], axis=0).astype(jnp.bfloat16)

        def first(t):
            code = jnp.concatenate(
                [xr[t * tile + s, pl.ds(m, 1), :] for s in range(tile)], axis=1)
            onehot = (number == code).astype(jnp.float32).astype(jnp.bfloat16)
            return reduce_rows(columns(t), onehot)

        total = over_tiles(first)
        before = cb[pl.ds(line, subdim), :]
        book = (total[:subdim] + lam * before) / (total[subdim:subdim + 1] + lam)
        norm = -jnp.sum(book * book, axis=0, keepdims=True)
        high = norm.astype(jnp.bfloat16).astype(jnp.float32)
        middle = (norm - high).astype(jnp.bfloat16).astype(jnp.float32)
        low = norm - high - middle
        center = jnp.concatenate(
            [2.0 * book.astype(jnp.bfloat16).astype(jnp.float32), high, middle, low,
             jnp.zeros((5, width), jnp.float32)], axis=0).T.astype(jnp.bfloat16)

        def second(t):
            points = columns(t)
            scores = jnp.dot(center, points, preferred_element_type=jnp.float32)
            top = jnp.max(scores, axis=0, keepdims=True)
            raised = jnp.exp(scores - top)
            share = 1.0 / jnp.sum(raised, axis=0, keepdims=True)
            return reduce_rows(points, (raised * share).astype(jnp.bfloat16))

        total = over_tiles(second)
        res[pl.ds(line, subdim), :] = (
            (total[:subdim] + lam * book) / (total[subdim:subdim + 1] + lam))
        return 0

    def forward(g):
        def one(source):
            result(source, source, g).wait_recv()
            passed(source, g).start()
        each_level(1, column, one)

    for g in groups:
        each_peer(lambda p, g=g: block(p, p, g).wait_recv())
        def several(i, _, g=g):
            for u in range(min(4, sizes[g])):
                train(starts[g] + i * min(4, sizes[g]) + u, 0)
            return 0
        lax.fori_loop(0, sizes[g] // min(4, sizes[g]), several, 0)
        if direct[g] or side == 1:
            each_peer(lambda p, g=g: result(me, p, g).start())
        else:
            each_level(1, column, lambda p, g=g: result(me, p, g).start())
            result(me, level * side + 1 - column, g).start()
        kept(g).start()
        if g > 0 and not direct[g - 1] and side == 2:
            forward(g - 1)
    if not direct[-1] and side == 2:
        forward(len(sizes) - 1)

    for g in groups:
        each_peer(lambda p, g=g: block(me, p, g).wait_send())
        if direct[g] or side == 1:
            each_peer(lambda p, g=g: result(me, p, g).wait_send())
            each_peer(lambda p, g=g: result(p, p, g).wait_recv())
        else:
            each_level(1, column, lambda p, g=g: result(me, p, g).wait_send())
            result(me, level * side + 1 - column, g).wait_send()
            each_level(1, column, lambda p, g=g: passed(p, g).wait_send())
            each_level(0, 1 - column, lambda p, g=g: result(p, p, g).wait_recv())
        kept(g).wait()


def shards(residuals, codes, codebook):
    rows = residuals.shape[0]
    local, subdim, width = codebook.shape
    n = lax.axis_size("rows")
    per = local // n
    parts = 4 if per % 4 == 0 else 1
    sizes = (per // parts,) * parts
    direct = (False,) * (parts - 1) + (True,)
    lam = rows * n / (8.0 * width)
    tile = min(n, 8)
    base = -(-per // 8) * 8
    held = base + per * subdim
    shape = (n, per * subdim, width)
    out = pl.pallas_call(
        functools.partial(kernel, n, sizes, direct, lam, tile),
        out_shape=pltpu.VMEM(shape, jnp.float32),
        in_specs=[pl.BlockSpec(memory_space=pl.ANY)] * 3,
        out_specs=pl.BlockSpec(memory_space=pltpu.VMEM),
        scratch_shapes=[
            pltpu.VMEM(residuals.shape, residuals.dtype),
            pltpu.VMEM(codes.shape, codes.dtype),
            pltpu.VMEM((n, held, rows), jnp.float32),
            pltpu.VMEM((n, held, rows), jnp.float32),
            pltpu.VMEM((per * subdim, width), jnp.float32),
            pltpu.VMEM((per * subdim, width), jnp.float32),
            pltpu.SemaphoreType.DMA((parts, n)),
            pltpu.SemaphoreType.DMA((parts, n)),
            pltpu.SemaphoreType.DMA((parts, n)),
            pltpu.SemaphoreType.DMA((parts, n)),
            pltpu.SemaphoreType.DMA((parts, n)),
            pltpu.SemaphoreType.DMA((parts,)),
            pltpu.SemaphoreType.DMA((3,)),
        ],
        compiler_params=pltpu.CompilerParams(collective_id=0, has_side_effects=True),
        name="lloyd",
    )(residuals, codes, codebook.reshape(shape))
    return out.reshape(local, subdim, width)


def solution(mesh):
    in_specs = (
        P(("groups", "rows"), "sub"),
        P(("groups", "rows"), "sub"),
        P(("groups", "sub"), None, None),
    )
    out_specs = P(("groups", "sub"), None, None)
    return jax.shard_map(shards, mesh=mesh, in_specs=in_specs, out_specs=out_specs, check_vma=False)
```

time: 211 us -> 34.7 us (0.16)
  waiting for transfers between devices: 149 us -> 0 us
  Pallas kernels: 0 us -> 33.8 us
  between operations: 13.5 us -> 0.01 us
  matrix products: 12.8 us -> 0 us
  local copies, waits for them, and re-layouts: 13.2 us -> 0.8 us
  loops' own time: 11.3 us -> 0 us
  other arithmetic: 10.6 us -> 0 us
    psum x2 -> x0, waiting for transfers between devices: 149 us -> none  [renew(): all_sums, all_counts = lax.psum((sums, counts), 'rows')]
    pallas_call x0 -> x1, Pallas kernels: none -> 33.8 us  [shards(): pl.pallas_call(functools.partial(kernel, n, sizes, direct, lam, tile), ou...]
    another operation x2 -> x0, loops' own time: 11.3 us -> none  [the longest x1 5.91 us: shards(): sums1, counts1 = lax.map(first, order)]
    dynamic_slice x24 -> x0, local copies, waits for them, and re-layouts: 10.2 us -> none  [the longest x16 10.1 us: shards(): sums1, counts1 = lax.map(first, order)]
    dot_general x16 -> x0, matrix products: 8.18 us -> none  [the longest x8 5.23 us: first(): jnp.einsum('gdr,grk->gdk', piece, onehot, preferred_element_type=jnp.floa...]
    reduce_sum x24 -> x0, other arithmetic: 5.9 us -> none  [the longest x8 2.85 us: first(): return (sums, jnp.sum(onehot, axis=1, dtype=jnp.float32))]
    sub x8 -> x0, matrix products: 4.64 us -> none  [second(): weights = jax.nn.softmax(scores, axis=-1).astype(jnp.bfloat16)]
    div x2 -> x0, other arithmetic: 3.02 us -> none  [renew(): return (all_sums + lam * prior) / (all_counts[:, None, :] + lam)]
  transfers between devices with their start and end apart: 2 -> 0, of which waited for: 2 -> 0; matrix products, arithmetic and copies ran while one was open for 0% -> 0% of each run, Pallas kernels for 0% -> 0%
where the time goes in v2:
time: 34.7 us; the launch traced here: 34.6 us
  Pallas kernels  33.8 us (97%)
  local copies, waits for them, and re-layouts  0.8 us (2%)
    pallas_call x1, Pallas kernels, shards(): pl.pallas_call(functools.partial(kernel, n, sizes, direct, lam, tile), ou...  33.8 us
    unnamed x1, local copies, waits for them, and re-layouts  0.8 us

profile of v2, /device:TPU:0, one launch (start us, length us, event | category | flops | bytes accessed | tf_op | source)
XLA Modules:
  0.0 34.6 jit_solution(1889292054660733153)
XLA Ops:
  0.0 33.8 %lloyd.1 = f32[8,128,128]{2,1,0:T(8,128)S(1)} custom-call(bf16[128,1024]{1,0:T(8,128)(2,1)} %x_hbm.1, s32[128,128]{1,0:T(8,128)} %c_hbm.1, f32[8,128,128]{2,1,0:T(8,128)} %bitcast.3), custom_call_target="tpu_custom_call" | custom-call | tf_op jit(solution)/shard_map/lloyd/pallas_call | solution.py:199
  33.8 0.8 %copy.5 = f32[128,8,128]{2,1,0:T(8,128)} copy(f32[128,8,128]{2,1,0:T(8,128)S(1)} %bitcast.2) | data formatting | bytes 1048576

commit v3 on v2

--- a/solution.py
+++ b/solution.py
@@ -18,10 +18,11 @@
     base = xs.shape[1] - per * subdim
     starts = [sum(sizes[:g]) for g in range(len(sizes))]
     groups = range(len(sizes))
-    side = 2 if n % 2 == 0 else 1
-    levels = n // side
+    half = n // 2
+    folds = n % 2 == 0
     me = lax.axis_index("rows")
-    level, column = lax.div(me, side), lax.rem(me, side)
+    twin = lax.rem(me + half, n)
+    near = lax.div(me, half) * half
 
     barrier = pltpu.get_barrier_semaphore()
 
@@ -70,11 +71,11 @@
             send_sem=send_o.at[g, target], recv_sem=recv_o.at[g, source],
             device_id={"rows": target}, device_id_type=MESH)
 
-    def passed(source, g):
+    def passed(target, g):
         return pltpu.make_async_remote_copy(
-            src_ref=o_ref.at[source, lines(g)], dst_ref=o_ref.at[source, lines(g)],
-            send_sem=relay.at[g, source], recv_sem=recv_o.at[g, source],
-            device_id={"rows": level * side + 1 - column}, device_id_type=MESH)
+            src_ref=o_ref.at[twin, lines(g)], dst_ref=o_ref.at[twin, lines(g)],
+            send_sem=relay.at[g, target], recv_sem=recv_o.at[g, twin],
+            device_id={"rows": target}, device_id_type=MESH)
 
     def kept(g):
         return pltpu.make_async_copy(res.at[lines(g)], o_ref.at[me, lines(g)], own.at[g])
@@ -83,13 +84,17 @@
         def body(k, _):
             act(lax.rem(me + k, n))
             return 0
-        lax.fori_loop(1, n, body, 0, unroll=n <= 8)
-
-    def each_level(first, where, act):
+        if n <= 8:
+            for k in sorted(range(1, n), key=lambda k: abs(2 * k - n)):
+                body(k, 0)
+        else:
+            lax.fori_loop(1, n, body, 0)
+
+    def each_near(act):
         def body(k, _):
-            act(lax.rem(level + k, levels) * side + where)
+            act(near + lax.rem(me - near + k, half))
             return 0
-        lax.fori_loop(first, levels, body, 0, unroll=n <= 8)
+        lax.fori_loop(1, half, body, 0, unroll=n <= 8)
 
     for g in groups:
         each_peer(lambda p, g=g: block(me, p, g).start())
@@ -108,38 +113,47 @@
         return lax.dot_general(points, weights, (((1,), (1,)), ((), ())),
                                preferred_element_type=jnp.float32)
 
+    def split(value):
+        high = value.astype(jnp.bfloat16).astype(jnp.float32)
+        middle = (value - high).astype(jnp.bfloat16).astype(jnp.float32)
+        return [high, middle, value - high - middle]
+
     def train(m, _):
         line = pl.multiple_of(m * subdim, subdim)
 
         def columns(t):
             parts = [xr[t * tile + s, pl.ds(base + line, subdim), :] for s in range(tile)]
             full = jnp.concatenate(parts, axis=1)
-            return jnp.concatenate([full, ones], axis=0).astype(jnp.bfloat16)
+            return jnp.concatenate([full, ones], axis=0)
 
         def first(t):
             code = jnp.concatenate(
                 [xr[t * tile + s, pl.ds(m, 1), :] for s in range(tile)], axis=1)
             onehot = (number == code).astype(jnp.float32).astype(jnp.bfloat16)
-            return reduce_rows(columns(t), onehot)
+            return reduce_rows(columns(t).astype(jnp.bfloat16), onehot)
 
         total = over_tiles(first)
         before = cb[pl.ds(line, subdim), :]
         book = (total[:subdim] + lam * before) / (total[subdim:subdim + 1] + lam)
-        norm = -jnp.sum(book * book, axis=0, keepdims=True)
-        high = norm.astype(jnp.bfloat16).astype(jnp.float32)
-        middle = (norm - high).astype(jnp.bfloat16).astype(jnp.float32)
-        low = norm - high - middle
+        scale = 1.4426950408889634
+        slope = (2.0 * scale) * book.astype(jnp.bfloat16).astype(jnp.float32)
+        norm = -scale * jnp.sum(book * book, axis=0, keepdims=True)
         center = jnp.concatenate(
-            [2.0 * book.astype(jnp.bfloat16).astype(jnp.float32), high, middle, low,
-             jnp.zeros((5, width), jnp.float32)], axis=0).T.astype(jnp.bfloat16)
+            split(slope) + split(norm) + [jnp.zeros((5, width), jnp.float32)],
+            axis=0).T.astype(jnp.bfloat16)
 
         def second(t):
-            points = columns(t)
+            full = columns(t)
+            points = jnp.concatenate([full[:subdim]] * 2 + [full], axis=0).astype(jnp.bfloat16)
             scores = jnp.dot(center, points, preferred_element_type=jnp.float32)
             top = jnp.max(scores, axis=0, keepdims=True)
-            raised = jnp.exp(scores - top)
+            raised = jnp.exp2(scores - top)
             share = 1.0 / jnp.sum(raised, axis=0, keepdims=True)
-            return reduce_rows(points, (raised * share).astype(jnp.bfloat16))
+            scaled = full * share
+            high = scaled.astype(jnp.bfloat16).astype(jnp.float32)
+            both = jnp.concatenate([high, scaled - high], axis=0).astype(jnp.bfloat16)
+            pair = reduce_rows(both, raised.astype(jnp.bfloat16))
+            return pair[:subdim + 8] + pair[subdim + 8:]
 
         total = over_tiles(second)
         res[pl.ds(line, subdim), :] = (
@@ -147,10 +161,8 @@
         return 0
 
     def forward(g):
-        def one(source):
-            result(source, source, g).wait_recv()
-            passed(source, g).start()
-        each_level(1, column, one)
+        result(twin, twin, g).wait_recv()
+        each_near(lambda p: passed(p, g).start())
 
     for g in groups:
         each_peer(lambda p, g=g: block(p, p, g).wait_recv())
@@ -159,27 +171,33 @@
                 train(starts[g] + i * min(4, sizes[g]) + u, 0)
             return 0
         lax.fori_loop(0, sizes[g] // min(4, sizes[g]), several, 0)
-        if direct[g] or side == 1:
+        if direct[g] or not folds:
             each_peer(lambda p, g=g: result(me, p, g).start())
         else:
-            each_level(1, column, lambda p, g=g: result(me, p, g).start())
-            result(me, level * side + 1 - column, g).start()
+            result(me, twin, g).start()
+            each_near(lambda p, g=g: result(me, p, g).start())
         kept(g).start()
-        if g > 0 and not direct[g - 1] and side == 2:
+        if g > 0 and not direct[g - 1] and folds:
             forward(g - 1)
-    if not direct[-1] and side == 2:
+    if not direct[-1] and folds:
         forward(len(sizes) - 1)
 
     for g in groups:
         each_peer(lambda p, g=g: block(me, p, g).wait_send())
-        if direct[g] or side == 1:
+        if direct[g] or not folds:
             each_peer(lambda p, g=g: result(me, p, g).wait_send())
             each_peer(lambda p, g=g: result(p, p, g).wait_recv())
         else:
-            each_level(1, column, lambda p, g=g: result(me, p, g).wait_send())
-            result(me, level * side + 1 - column, g).wait_send()
-            each_level(1, column, lambda p, g=g: passed(p, g).wait_send())
-            each_level(0, 1 - column, lambda p, g=g: result(p, p, g).wait_recv())
+            result(me, twin, g).wait_send()
+            each_near(lambda p, g=g: result(me, p, g).wait_send())
+            each_near(lambda p, g=g: passed(p, g).wait_send())
+            each_near(lambda p, g=g: result(p, p, g).wait_recv())
+
+            def across(p, g=g):
+                q = lax.rem(p + half, n)
+                result(q, q, g).wait_recv()
+
+            each_near(across)
         kept(g).wait()
 
 

time: 34.7 us -> 32.8 us (0.945)
  Pallas kernels: 33.8 us -> 31.9 us
    pallas_call x1, Pallas kernels: 33.8 us -> 31.9 us  [shards(): pl.pallas_call(functools.partial(kernel, n, sizes, direct, lam, tile), ou...]
where the time goes in v3:
time: 32.8 us; the launch traced here: 32.7 us
  Pallas kernels  31.9 us (97%)
  local copies, waits for them, and re-layouts  0.8 us (2%)
    pallas_call x1, Pallas kernels, shards(): pl.pallas_call(functools.partial(kernel, n, sizes, direct, lam, tile), ou...  31.9 us
    unnamed x1, local copies, waits for them, and re-layouts  0.8 us

profile of v3, /device:TPU:0, one launch (start us, length us, event | category | flops | bytes accessed | tf_op | source)
XLA Modules:
  0.0 32.7 jit_solution(13392758617293913414)
XLA Ops:
  0.0 31.9 %lloyd.1 = f32[8,128,128]{2,1,0:T(8,128)S(1)} custom-call(bf16[128,1024]{1,0:T(8,128)(2,1)} %x_hbm.1, s32[128,128]{1,0:T(8,128)} %c_hbm.1, f32[8,128,128]{2,1,0:T(8,128)} %bitcast.3), custom_call_target="tpu_custom_call" | custom-call | tf_op jit(solution)/shard_map/lloyd/pallas_call | solution.py:217
  31.9 0.8 %copy.5 = f32[128,8,128]{2,1,0:T(8,128)} copy(f32[128,8,128]{2,1,0:T(8,128)S(1)} %bitcast.2) | data formatting | bytes 1048576
